TPU v7x, 32 devices: a whole 2x2x4 slice. The times are simulated.
32 devices in a mesh: gx: 4 (over z), gy: 8 (over y, x, core).
Axes of the slice: x: 2, y: 2, z: 4, core: 2. Of those that a mesh axis runs over, the one named last changes fastest.
Arguments:
- conductivity: float32 [128, 256, 128], P('gx', 'gy'), may hold values from 0.25 to 4
- source: float32 [128, 256, 128], P('gx', 'gy'), may hold values from -12 to 12
- initial: float32 [128, 256, 128], P('gx', 'gy'), may hold values from -3 to 3
Outputs:
- solution: float32 [128, 256, 128], P('gx', 'gy')
All inputs are finite; a program needn't handle non-finite values.
Results may differ from a plain program's by a relative error of at most 0.0003.
Values sent between devices are 32-bit elements; how exact they have to be, the bound alone decides.
A program may use at most 64 MiB of HBM per device.

v0:
```python
import jax
import jax.numpy as jnp
from jax import lax
from jax.sharding import PartitionSpec as P

NU = 3
CG_ITERS = 32


relax_weight = 0.8


def extended(cells, sides, width):
    for axis, dim in sides:
        count = lax.axis_size(axis)
        ends = count - 1
        head = lax.slice_in_dim(cells, 0, width, axis=dim)
        tail = lax.slice_in_dim(cells, cells.shape[dim] - width, cells.shape[dim], axis=dim)
        cells = jnp.concatenate(
            [
                lax.ppermute(tail, axis, [(i, (i + 1) % count) for i in range(ends)]),
                cells,
                lax.ppermute(head, axis, [((i + 1) % count, i) for i in range(ends)]),
            ],
            axis=dim,
        )
    return cells


def operate(padded, cond_pad):
    center_cond = cond_pad[1:-1, 1:-1]
    center = padded[1:-1, 1:-1]
    face_east = 0.5 * (center_cond + cond_pad[2:, 1:-1])
    face_west = 0.5 * (center_cond + cond_pad[:-2, 1:-1])
    face_north = 0.5 * (center_cond + cond_pad[1:-1, 2:])
    face_south = 0.5 * (center_cond + cond_pad[1:-1, :-2])
    between = 0.5 * (center_cond[:, :, 1:] + center_cond[:, :, :-1])
    zero_plane = jnp.zeros(center.shape[:2] + (1,), center.dtype)
    face_up = jnp.concatenate([between, zero_plane], 2)
    face_down = jnp.concatenate([zero_plane, between], 2)
    value_up = jnp.concatenate([center[:, :, 1:], zero_plane], 2)
    value_down = jnp.concatenate([zero_plane, center[:, :, :-1]], 2)
    diagonal = face_east + face_west + face_north + face_south + face_up + face_down
    neighbor_sum = (
        face_east * padded[2:, 1:-1]
        + face_west * padded[:-2, 1:-1]
        + face_north * padded[1:-1, 2:]
        + face_south * padded[1:-1, :-2]
        + face_up * value_up
        + face_down * value_down
    )
    return (diagonal * center - neighbor_sum, diagonal, center_cond, center)


def smooth_once(padded, cond_pad, source):
    applied, diagonal, center_cond, center = operate(padded, cond_pad)
    inside = center_cond > 0
    update = relax_weight * (source - applied) / jnp.where(inside, diagonal, 1.0)
    return jnp.where(inside, center + update, 0.0)


def coarse_apply(estimate, coarse_diag, flow_east, flow_north):
    edge_rows = jnp.zeros((1, estimate.shape[1]), estimate.dtype)
    edge_cols = jnp.zeros((estimate.shape[0], 1), estimate.dtype)
    ahead_x = jnp.concatenate([estimate[1:], edge_rows], 0)
    carried_x = flow_east * estimate
    behind_x = jnp.concatenate([edge_rows, carried_x[:-1]], 0)
    ahead_y = jnp.concatenate([estimate[:, 1:], edge_cols], 1)
    carried_y = flow_north * estimate
    behind_y = jnp.concatenate([edge_cols, carried_y[:, :-1]], 1)
    return coarse_diag * estimate - flow_east * ahead_x - behind_x - flow_north * ahead_y - behind_y


def coarse_solve(coarse_source, coarse_diag, flow_east, flow_north):

    def iterate_once(counter, carried):
        estimate, remainder, search, norm_now = carried
        product = coarse_apply(search, coarse_diag, flow_east, flow_north)
        alpha_step = norm_now / jnp.sum(search * product)
        estimate = estimate + alpha_step * search
        remainder = remainder - alpha_step * product
        norm_next = jnp.sum(remainder * remainder)
        search = remainder + norm_next / norm_now * search
        return (estimate, remainder, search, norm_next)

    start_state = (
        jnp.zeros_like(coarse_source),
        coarse_source,
        coarse_source,
        jnp.sum(coarse_source * coarse_source),
    )
    return lax.fori_loop(0, CG_ITERS, iterate_once, start_state)[0]


def trim_rim(array, width, depth):
    cut = depth - width
    return array[cut : array.shape[0] - cut, cut : array.shape[1] - cut]


def relax_deep(padded, width, cond_big, source_big, sweeps, depth):
    for repeat in range(sweeps):
        current = width - repeat
        padded = smooth_once(
            padded, trim_rim(cond_big, current, depth), trim_rim(source_big, current - 1, depth)
        )
    return padded


def body(conductivity, source, initial):
    extent_x = conductivity.shape[0]
    extent_y = conductivity.shape[1]
    depth = NU + 1
    stacked = extended(jnp.stack([conductivity, source, initial]), (("gx", 1), ("gy", 2)), depth)
    padded = relax_deep(stacked[2], depth, stacked[0], stacked[1], NU, depth)
    cond_pad = trim_rim(stacked[0], 1, depth)
    applied = operate(padded, cond_pad)[0]
    iterate = padded[1:-1, 1:-1]
    remainder = source - applied
    coarse_source = jnp.sum(remainder).reshape(1)
    flow_east = jnp.sum(0.5 * (cond_pad[extent_x, 1:-1] + cond_pad[extent_x + 1, 1:-1])).reshape(1)
    flow_west = jnp.sum(0.5 * (cond_pad[1, 1:-1] + cond_pad[0, 1:-1])).reshape(1)
    flow_north = jnp.sum(0.5 * (cond_pad[1:-1, extent_y] + cond_pad[1:-1, extent_y + 1])).reshape(1)
    flow_south = jnp.sum(0.5 * (cond_pad[1:-1, 1] + cond_pad[1:-1, 0])).reshape(1)
    coarse_diag = flow_east + flow_west + flow_north + flow_south
    gathered = (
        lax.all_gather(coarse_source, ("gx", "gy"), axis=0, tiled=True),
        lax.all_gather(coarse_diag, ("gx", "gy"), axis=0, tiled=True),
        lax.all_gather(flow_east, ("gx", "gy"), axis=0, tiled=True),
        lax.all_gather(flow_north, ("gx", "gy"), axis=0, tiled=True),
    )
    count_x = lax.axis_size("gx")
    count_y = lax.axis_size("gy")
    correction = coarse_solve(
        gathered[0].reshape(count_x, count_y),
        gathered[1].reshape(count_x, count_y),
        gathered[2].reshape(count_x, count_y),
        gathered[3].reshape(count_x, count_y),
    )
    index_x = lax.axis_index("gx")
    index_y = lax.axis_index("gy")
    own_share = lax.dynamic_slice(correction, (index_x, index_y), (1, 1))[0, 0]
    iterate = iterate + own_share
    refreshed = extended(iterate, (("gx", 0), ("gy", 1)), NU)
    iterate = relax_deep(refreshed, NU, stacked[0], stacked[1], NU, depth)
    return iterate


def solution(mesh):
    return jax.shard_map(
        body,
        mesh=mesh,
        in_specs=(P("gx", "gy", None), P("gx", "gy", None), P("gx", "gy", None)),
        out_specs=P("gx", "gy", None),
        check_vma=False,
    )
```

profile of v0, /device:TPU:12, one launch (start us, length us, event | category | flops | bytes accessed | tf_op | source)
XLA Modules:
  0.0 251.2 jit_solution(3323048129929847691)
XLA Ops:
  1.2 2.4 collective-permute-start.1
  3.5 3.5 %collective-permute-start = (f32[3,4,32,128]{3,2,1,0:T(8,128)S(1)}, f32[3,4,32,128]{3,2,1,0:T(8,128)S(1)}, u32[]{:S(2)}, u32[]{:S(2)}) collective-permute-start(f32[3,4,32,128]{3,2,1,0:T(8,128)S(1)} %get-tuple-element.116), channel_id=1, source_target_pairs={{0,8},{8,16},{16,24},{1,9},{9,17},{17,25},{2,10},{10,18},{18,26},{... | collective-permute-start | bytes 589832 | tf_op jit(solution)/shard_map/ppermute | solution.py:21
  7.0 2.7 %collective-permute-done.1 = f32[3,4,32,128]{3,2,1,0:T(8,128)S(1)} collective-permute-done((f32[3,4,32,128]{3,2,1,0:T(8,128)S(1)}, f32[3,4,32,128]{3,2,1,0:T(8,128)S(1)}, u32[]{:S(2)}, u32[]{:S(2)}) %collective-permute-start.1) | collective-permute-done | bytes 196640 | tf_op jit(solution)/shard_map/ppermute | solution.py:23
  9.7 2.1 collective-permute-done
  11.8 1.3 pad_maximum_fusion.6
  13.1 1.9 collective-permute-start.3
  15.0 2.4 collective-permute-start.2
  17.4 1.3 collective-permute-done.3
  18.7 4.7 %collective-permute-done.2 = f32[3,40,4,128]{3,2,1,0:T(4,128)S(1)} collective-permute-done((f32[3,40,4,128]{3,2,1,0:T(4,128)S(1)}, f32[3,40,4,128]{3,2,1,0:T(4,128)S(1)}, u32[]{:S(2)}, u32[]{:S(2)}) %collective-permute-start.2) | collective-permute-done | bytes 245792 | tf_op jit(solution)/shard_map/ppermute | solution.py:21
  26.6 1.3 fusion.8
  28.2 2.0 fusion.35
  30.4 1.9 fusion.63
  32.5 1.4 fusion.88
  36.1 2.5 add_dynamic-update-slice_fusion
  38.6 40.3 %all-reduce.30 = (f32[32]{0:T(128)S(1)}, f32[32]{0:T(128)S(1)}, f32[32]{0:T(128)S(1)}, f32[32]{0:T(128)S(1)}) all-reduce(f32[32]{0:T(128)S(1)} %dynamic-update-slice, f32[32]{0:T(128)S(1)} %add_dynamic-update-slice_fusion, f32[32]{0:T(128)S(1)} %dynamic-update-slice.2, ...), channel_id=1, replica_groups=mesh['gx'=4,'gy'=8] {'gx','gy'}, use_global_device_ids=true, to_apply=%add.26 | all-reduce | flops 128 | bytes 1024
  79.8 145.4 %while.17 = (s32[]{:T(128)}, f32[4,8]{1,0:T(4,128)}, f32[4,8]{1,0:T(4,128)S(1)}, f32[4,8]{1,0:T(4,128)S(1)}, f32[]{:T(128)}, /*index=5*/f32[4,8]{1,0:T(4,128)S(1...) while((s32[]{:T(128)}, f32[4,8]{1,0:T(4,128)}, f32[4,8]{1,0:T(4,128)S(1)}, ...), condition=%wide.region_9.10_spmd.clone, body=%wide.region_6.9_spmd.clone.sunk | while | flops 643 | bytes 3307 | solution.py:92
  87.0 1.3 multiply_add_fusion.2
  91.6 1.3 multiply_add_fusion.2
  119.0 1.3 multiply_add_fusion.2
  146.3 1.3 multiply_add_fusion.2
  150.9 1.3 multiply_add_fusion.2
  173.7 1.3 multiply_add_fusion.2
  225.2 1.3 dynamic_slice.3
  227.3 2.4 collective-permute-start.5
  229.8 3.5 %collective-permute-start.4 = (f32[3,32,128]{2,1,0:T(8,128)S(1)}, f32[3,32,128]{2,1,0:T(8,128)S(1)}, u32[]{:S(2)}, u32[]{:S(2)}) collective-permute-start(f32[3,32,128]{2,1,0:T(8,128)S(1)} %get-tuple-element.134), channel_id=1, source_target_pairs={{0,8},{8,16},{16,24},{1,9},{9,17},{17,25},{2,10},{10,18},{18,26},{... | collective-permute-start | bytes 147464 | tf_op jit(solution)/shard_map/ppermute | solution.py:21
  233.3 2.6 %collective-permute-done.4 = f32[3,32,128]{2,1,0:T(8,128)S(1)} collective-permute-done((f32[3,32,128]{2,1,0:T(8,128)S(1)}, f32[3,32,128]{2,1,0:T(8,128)S(1)}, u32[]{:S(2)}, u32[]{:S(2)}) %collective-permute-start.4) | collective-permute-done | bytes 49184 | tf_op jit(solution)/shard_map/ppermute | solution.py:21
  235.9 1.9 collective-permute-start.7
  237.8 2.6 %collective-permute-start.6 = (f32[38,3,128]{2,1,0:T(4,128)S(1)}, f32[38,3,128]{2,1,0:T(4,128)S(1)}, u32[]{:S(2)}, u32[]{:S(2)}) collective-permute-start(f32[38,3,128]{2,1,0:T(4,128)S(1)} %get-tuple-element.132), channel_id=1, source_target_pairs={{0,1},{1,2},{2,3},{3,4},{4,5},{5,6},{6,7},{8,9},{9,10},{10,11},{11... | collective-permute-start | bytes 175112 | tf_op jit(solution)/shard_map/ppermute | solution.py:21
  240.4 4.0 %collective-permute-done.6 = f32[38,3,128]{2,1,0:T(4,128)S(1)} collective-permute-done((f32[38,3,128]{2,1,0:T(4,128)S(1)}, f32[38,3,128]{2,1,0:T(4,128)S(1)}, u32[]{:S(2)}, u32[]{:S(2)}) %collective-permute-start.6) | collective-permute-done | bytes 58400 | tf_op jit(solution)/shard_map/ppermute | solution.py:21
  244.9 1.4 fusion.24
  247.1 1.3 fusion.52
  249.4 1.7 fusion.80
  (239 shorter events, 88.1 us)
Async XLA Ops:
  0.0 23.4 %copy-start.3 = (f32[32,32,128]{2,1,0:T(8,128)S(1)}, f32[32,32,128]{2,1,0:T(8,128)}, u32[]{:S(2)}) copy-start(f32[32,32,128]{2,1,0:T(8,128)} %param.7) | copy-start | bytes 1572868
  0.0 23.4 %copy-start = (f32[32,32,128]{2,1,0:T(8,128)S(1)}, f32[32,32,128]{2,1,0:T(8,128)}, u32[]{:S(2)}) copy-start(f32[32,32,128]{2,1,0:T(8,128)} %param.6) | copy-start | bytes 1572868
  0.0 23.4 %copy-start.4 = (f32[32,32,128]{2,1,0:T(8,128)S(1)}, f32[32,32,128]{2,1,0:T(8,128)}, u32[]{:S(2)}) copy-start(f32[32,32,128]{2,1,0:T(8,128)} %param.5) | copy-start | bytes 1572868
  1.2 8.5 %collective-permute-start.1 = (f32[3,4,32,128]{3,2,1,0:T(8,128)S(1)}, f32[3,4,32,128]{3,2,1,0:T(8,128)S(1)}, u32[]{:S(2)}, u32[]{:S(2)}) collective-permute-start(f32[3,4,32,128]{3,2,1,0:T(8,128)S(1)} %get-tuple-element.117), channel_id=1, source_target_pairs={{8,0},{16,8},{24,16},{9,1},{17,9},{25,17},{10,2},{18,10},{26,18},{... | collective-permute-start | bytes 589832 | tf_op jit(solution)/shard_map/ppermute | solution.py:23
  3.5 8.3 %collective-permute-start = (f32[3,4,32,128]{3,2,1,0:T(8,128)S(1)}, f32[3,4,32,128]{3,2,1,0:T(8,128)S(1)}, u32[]{:S(2)}, u32[]{:S(2)}) collective-permute-start(f32[3,4,32,128]{3,2,1,0:T(8,128)S(1)} %get-tuple-element.116), channel_id=1, source_target_pairs={{0,8},{8,16},{16,24},{1,9},{9,17},{17,25},{2,10},{10,18},{18,26},{... | collective-permute-start | bytes 589832 | tf_op jit(solution)/shard_map/ppermute | solution.py:21
  13.1 5.6 %collective-permute-start.3 = (f32[3,40,4,128]{3,2,1,0:T(4,128)S(1)}, f32[3,40,4,128]{3,2,1,0:T(4,128)S(1)}, u32[]{:S(2)}, u32[]{:S(2)}) collective-permute-start(f32[3,40,4,128]{3,2,1,0:T(4,128)S(1)} %get-tuple-element.115), channel_id=1, source_target_pairs={{1,0},{2,1},{3,2},{4,3},{5,4},{6,5},{7,6},{9,8},{10,9},{11,10},{12... | collective-permute-start | bytes 737288 | tf_op jit(solution)/shard_map/ppermute | solution.py:23
  15.0 8.4 %collective-permute-start.2 = (f32[3,40,4,128]{3,2,1,0:T(4,128)S(1)}, f32[3,40,4,128]{3,2,1,0:T(4,128)S(1)}, u32[]{:S(2)}, u32[]{:S(2)}) collective-permute-start(f32[3,40,4,128]{3,2,1,0:T(4,128)S(1)} %get-tuple-element.114), channel_id=1, source_target_pairs={{0,1},{1,2},{2,3},{3,4},{4,5},{5,6},{6,7},{8,9},{9,10},{10,11},{11... | collective-permute-start | bytes 737288 | tf_op jit(solution)/shard_map/ppermute | solution.py:21
  24.3 3.9 %copy-start.1 = (f32[36,36,127]{2,1,0:T(8,128)}, f32[36,36,127]{2,1,0:T(8,128)S(1)}, u32[]{:S(2)}) copy-start(f32[36,36,127]{2,1,0:T(8,128)S(1)} %fusion.38) | copy-start | bytes 1975108
  24.8 7.7 %copy-start.5 = (f32[32,32,127]{2,1,0:T(8,128)}, f32[32,32,127]{2,1,0:T(8,128)S(1)}, u32[]{:S(2)}) copy-start(f32[32,32,127]{2,1,0:T(8,128)S(1)} %fusion.91) | copy-start | bytes 1560580
  227.3 6.0 %collective-permute-start.5 = (f32[3,32,128]{2,1,0:T(8,128)S(1)}, f32[3,32,128]{2,1,0:T(8,128)S(1)}, u32[]{:S(2)}, u32[]{:S(2)}) collective-permute-start(f32[3,32,128]{2,1,0:T(8,128)S(1)} %get-tuple-element.135), channel_id=1, source_target_pairs={{8,0},{16,8},{24,16},{9,1},{17,9},{25,17},{10,2},{18,10},{26,18},{... | collective-permute-start | bytes 147464 | tf_op jit(solution)/shard_map/ppermute | solution.py:23
  229.7 15.1 %copy-start.2 = (f32[36,36,127]{2,1,0:T(8,128)S(1)}, f32[36,36,127]{2,1,0:T(8,128)}, u32[]{:S(2)}) copy-start(f32[36,36,127]{2,1,0:T(8,128)} %copy-done.1) | copy-start | bytes 1975108
  229.8 15.1 %copy-start.7 = (pred[36,36,128]{2,1,0:T(8,128)(4,1)S(1)}, pred[36,36,128]{2,1,0:T(8,128)(4,1)}, u32[]{:S(2)}) copy-start(pred[36,36,128]{2,1,0:T(8,128)(4,1)} %get-tuple-element.106) | copy-start | bytes 497668
  229.8 6.1 %collective-permute-start.4 = (f32[3,32,128]{2,1,0:T(8,128)S(1)}, f32[3,32,128]{2,1,0:T(8,128)S(1)}, u32[]{:S(2)}, u32[]{:S(2)}) collective-permute-start(f32[3,32,128]{2,1,0:T(8,128)S(1)} %get-tuple-element.134), channel_id=1, source_target_pairs={{0,8},{8,16},{16,24},{1,9},{9,17},{17,25},{2,10},{10,18},{18,26},{... | collective-permute-start | bytes 147464 | tf_op jit(solution)/shard_map/ppermute | solution.py:21
  235.9 4.5 %collective-permute-start.7 = (f32[38,3,128]{2,1,0:T(4,128)S(1)}, f32[38,3,128]{2,1,0:T(4,128)S(1)}, u32[]{:S(2)}, u32[]{:S(2)}) collective-permute-start(f32[38,3,128]{2,1,0:T(4,128)S(1)} %get-tuple-element.133), channel_id=1, source_target_pairs={{1,0},{2,1},{3,2},{4,3},{5,4},{6,5},{7,6},{9,8},{10,9},{11,10},{12... | collective-permute-start | bytes 175112 | tf_op jit(solution)/shard_map/ppermute | solution.py:23
  237.8 6.6 %collective-permute-start.6 = (f32[38,3,128]{2,1,0:T(4,128)S(1)}, f32[38,3,128]{2,1,0:T(4,128)S(1)}, u32[]{:S(2)}, u32[]{:S(2)}) collective-permute-start(f32[38,3,128]{2,1,0:T(4,128)S(1)} %get-tuple-element.132), channel_id=1, source_target_pairs={{0,1},{1,2},{2,3},{3,4},{4,5},{5,6},{6,7},{8,9},{9,10},{10,11},{11... | collective-permute-start | bytes 175112 | tf_op jit(solution)/shard_map/ppermute | solution.py:21
  246.2 0.9 copy-start.8
  248.4 1.0 copy-start.6
where the time goes:
time: 253 us; the launch traced here: 251 us
  other arithmetic  102 us (40%)
  loops' own time  61 us (24%)
  blocking collectives  40.3 us (16%)
  starting transfers between devices  20.7 us (8%)
  waiting for transfers between devices  17.3 us (7%)
  local copies, waits for them, and re-layouts  9.3 us (4%)
    another operation x1, loops' own time, coarse_solve(): return lax.fori_loop(0, CG_ITERS, iterate_once, start_state)[0]  61 us
    unnamed x1, blocking collectives  40.3 us
    add x32, other arithmetic, iterate_once(): search = remainder + norm_next / norm_now * search  39.7 us
    reduce_sum x32, other arithmetic, iterate_once(): alpha_step = norm_now / jnp.sum(search * product)  21.7 us
    reduce_sum x32, other arithmetic, iterate_once(): norm_next = jnp.sum(remainder * remainder)  20.4 us
    ppermute x4, waiting for transfers between devices, extended(): lax.ppermute(tail, axis, [(i, (i + 1) % count) for i in range(ends)])  13.4 us
    ppermute x4, starting transfers between devices, extended(): lax.ppermute(tail, axis, [(i, (i + 1) % count) for i in range(ends)])  12 us
    select_n x6, other arithmetic, smooth_once(): return jnp.where(inside, center + update, 0.0)  9.46 us
  transfers between devices with their start and end apart: 8, of which 6 were waited for; matrix products, arithmetic and copies ran while one was open for 0% of the time, Pallas kernels for 0%

commit v1 on v0

v1 whole, which is shorter than its diff:
```python
import functools

import jax
import jax.numpy as jnp
from jax import lax
from jax.experimental import pallas as pl
from jax.experimental.pallas import tpu as pltpu
from jax.sharding import PartitionSpec as P

NU = 3
CG_ITERS = 32
H = NU + 1

relax_weight = 0.8
MESH = pl.DeviceIdType.MESH
DIRS = [(1, 0), (-1, 0), (0, 1), (0, -1), (1, 1), (1, -1), (-1, 1), (-1, -1)]


def inside(ix, iy, cx, cy):
    return (ix >= 0) & (ix < cx) & (iy >= 0) & (iy < cy)


def rows_loop(lo, hi, step, carry):
    count = hi - lo
    pairs = count // 2

    def two(i, c):
        x = lo + 2 * i
        return step(x + 1, step(x, c))

    carry = lax.fori_loop(0, pairs, two, carry)
    if count % 2:
        carry = step(hi - 1, carry)
    return carry


def kernel(cx, cy, nx, ny, *refs):
    (k_in, f_in, u_in, k4, f4, u4, out,
     K, F, U, V, CE, CN, CU, W, YLO, YHI,
     XLO2, XHI2, YLO2, YHI2, PLO, PHI, GC, GS, E,
     lsem, osem, ssem, rsem, ssem2, rsem2,
     c1s, c1r, c2s, c2r, s1s, s1r, s2s, s2r) = refs
    X = nx + 2 * H
    Y = ny + 2 * H
    ix = lax.axis_index("gx")
    iy = lax.axis_index("gy")
    full = [k_in, f_in, u_in]
    quad = [k4, f4, u4]
    ext = [K, F, U]

    barrier = pltpu.get_barrier_semaphore()

    def greet_x(k, c):
        pl.semaphore_signal(barrier, inc=1, device_id=(lax.rem(ix + k, cx), iy), device_id_type=MESH)
        return c

    def greet_y(k, c):
        pl.semaphore_signal(barrier, inc=1, device_id=(ix, lax.rem(iy + k, cy)), device_id_type=MESH)
        return c

    lax.fori_loop(1, cx, greet_x, 0)
    lax.fori_loop(1, cy, greet_y, 0)
    for dx, dy in DIRS[4:]:
        @pl.when(inside(ix + dx, iy + dy, cx, cy))
        def _(dx=dx, dy=dy):
            pl.semaphore_signal(barrier, inc=1, device_id=(ix + dx, iy + dy), device_id_type=MESH)

    local = [pltpu.make_async_copy(full[a], ext[a].at[H:H + nx, 0:ny, :], lsem.at[a]) for a in range(3)]
    for copy in local:
        copy.start()

    sides_x = (ix > 0).astype(jnp.int32) + (ix < cx - 1).astype(jnp.int32)
    sides_y = (iy > 0).astype(jnp.int32) + (iy < cy - 1).astype(jnp.int32)
    pl.semaphore_wait(barrier, (cx - 1) + (cy - 1) + sides_x * sides_y)

    def halo(a, d):
        dx, dy = DIRS[d]
        slot = a * 8 + d
        src_rows = {1: (nx - H, nx), -1: (0, H), 0: (0, nx)}[dx]
        dst_rows = {1: (0, H), -1: (X - H, X), 0: (H, H + nx)}[dx]
        if dy == 0:
            src = full[a].at[src_rows[0]:src_rows[1]]
            dst = ext[a].at[dst_rows[0]:dst_rows[1], 0:ny, :]
        else:
            src = quad[a].at[src_rows[0]:src_rows[1], ny // H - 1 if dy == 1 else 0]
            dst = (YLO if dy == 1 else YHI).at[a, dst_rows[0]:dst_rows[1]]
        return pltpu.make_async_remote_copy(
            src_ref=src, dst_ref=dst, send_sem=ssem.at[slot], recv_sem=rsem.at[slot],
            device_id=(ix + dx, iy + dy), device_id_type=MESH)

    def each(d, sign, act):
        dx, dy = DIRS[d]
        pl.when(inside(ix + sign * dx, iy + sign * dy, cx, cy))(act)

    for d in range(8):
        def start(d=d):
            for a in range(3):
                halo(a, d).start()
        each(d, 1, start)

    def clear_when_absent(d):
        dx, dy = DIRS[d]
        rows = {1: (0, H), -1: (X - H, X), 0: (H, H + nx)}[dx]

        @pl.when(jnp.logical_not(inside(ix - dx, iy - dy, cx, cy)))
        def _():
            if dy == 0:
                for a in range(3):
                    ext[a][rows[0]:rows[1], 0:ny, :] = jnp.zeros((H, ny, 128), jnp.float32)
                (XLO2 if dx == 1 else XHI2)[...] = jnp.zeros((NU, ny, 128), jnp.float32)
            else:
                wide = YLO if dy == 1 else YHI
                wide2 = YLO2 if dy == 1 else YHI2
                for a in range(3):
                    wide[a, rows[0]:rows[1]] = jnp.zeros((rows[1] - rows[0], H, 128), jnp.float32)
                wide2[rows[0]:rows[1]] = jnp.zeros((rows[1] - rows[0], H, 128), jnp.float32)

    for d in range(8):
        clear_when_absent(d)

    for copy in local:
        copy.wait()

    f_total = rows_loop(H, H + nx, lambda x, c: c + F[x, 0:ny, :], jnp.zeros((ny, 128), jnp.float32))

    for d in range(8):
        def finish(d=d):
            for a in range(3):
                halo(a, d).wait_recv()
        each(d, -1, finish)

    def unpack(x, c):
        for a in range(3):
            ext[a][x, ny:ny + H, :] = YHI[a, x]
            ext[a][x, ny + H:Y, :] = YLO[a, x]
        return c

    rows_loop(0, X, unpack, 0)

    lane = lax.broadcasted_iota(jnp.int32, (Y, 128), 1)
    up_half = jnp.where(lane < 127, 0.5, 0.0)

    def next_y(v):
        return pltpu.roll(v, Y - 1, 0)

    def last_y(v):
        return pltpu.roll(v, 1, 0)

    def next_z(v):
        return pltpu.roll(v, 127, 1)

    def last_z(v):
        return pltpu.roll(v, 1, 1)

    def faces(x, c):
        k, west, total = c
        k_next = K[x + 1]
        east = 0.5 * (k + k_next)
        north = 0.5 * (k + next_y(k))
        up = up_half * (k + next_z(k))
        d = east + west + north + last_y(north) + up + last_z(up)
        CE[x] = east
        CN[x] = north
        CU[x] = up
        W[x] = jnp.where(k > 0, relax_weight / jnp.where(k > 0, d, 1.0), 0.0)
        return k_next, east, total + north

    k1 = K[1]
    first = 0.5 * (K[0] + k1)
    CE[0] = first
    zero = jnp.zeros((Y, 128), jnp.float32)
    carry = rows_loop(1, H, faces, (k1, first, zero))
    carry = rows_loop(H, H + nx, faces, (carry[0], carry[1], zero))
    north_total = carry[2]
    rows_loop(H + nx, X - 1, faces, carry)

    def whole_sum(v):
        return jnp.sum(jnp.sum(v, axis=0, keepdims=True), axis=1, keepdims=True)

    flow_e = whole_sum(CE[X - H - 1, 0:ny, :])
    flow_w = whole_sum(CE[H - 1, 0:ny, :])
    flow_n = whole_sum(north_total[ny - 1:ny])
    flow_s = whole_sum(north_total[Y - 1:Y])
    coarse_diag = flow_e + flow_w + flow_n + flow_s
    GC[iy, ix, 0:1, :] = jnp.broadcast_to(coarse_diag, (1, 128))
    GC[iy, ix, 1:2, :] = jnp.broadcast_to(flow_e, (1, 128))
    GC[iy, ix, 2:3, :] = jnp.broadcast_to(flow_n, (1, 128))
    GC[iy, ix, 3:4, :] = jnp.zeros((1, 128), jnp.float32)

    def along_x(G, ss, rs):
        def of(k):
            return pltpu.make_async_remote_copy(
                src_ref=G.at[iy, ix], dst_ref=G.at[iy, ix], send_sem=ss.at[k - 1], recv_sem=rs.at[k - 1],
                device_id=(lax.rem(ix + k, cx), iy), device_id_type=MESH)
        return of

    def along_y(G, ss, rs):
        def of(k):
            return pltpu.make_async_remote_copy(
                src_ref=G.at[iy], dst_ref=G.at[iy], send_sem=ss.at[k - 1], recv_sem=rs.at[k - 1],
                device_id=(ix, lax.rem(iy + k, cy)), device_id_type=MESH)
        return of

    def run(of, count, method):
        def go(k, c):
            getattr(of(k), method)()
            return c
        lax.fori_loop(1, count, go, 0)

    coef_x, coef_y = along_x(GC, c1s, c1r), along_y(GC, c2s, c2r)
    sum_x, sum_y = along_x(GS, s1s, s1r), along_y(GS, s2s, s2r)
    run(coef_x, cx, "start")

    def sweep(src, dst, lo, hi, final=None):
        def step(x, c):
            u, west, total = c
            u_next = src[x + 1]
            east = CE[x] * (u_next - u)
            cn = CN[x]
            north = cn * (next_y(u) - u)
            up = CU[x] * (next_z(u) - u)
            change = (east - west) + (north - last_y(north)) + (up - last_z(up))
            new = u + W[x] * (F[x] + change)
            dst[x] = new
            if final is not None:
                total = total + cn * (next_y(new) - new)
            return u_next, east, total
        u = src[lo]
        west = CE[lo - 1] * (u - src[lo - 1])
        zero = jnp.zeros((Y, 128), jnp.float32) if final is not None else 0
        if final is None:
            rows_loop(lo, hi, step, (u, west, zero))
            return None
        carry = rows_loop(lo, final[0], step, (u, west, zero))
        carry = rows_loop(final[0], final[1], step, (carry[0], carry[1], zero))
        rows_loop(final[1], hi, step, carry)
        return carry[2]

    sweep(U, V, 1, X - 1)
    run(coef_x, cx, "wait_recv")
    run(coef_y, cy, "start")
    sweep(V, U, 2, X - 2)
    y_total = sweep(U, V, 3, X - 3, (H, H + nx))

    low, high = H - 1, X - H - 1
    x_total = (CE[high, 0:ny, :] * (V[high + 1, 0:ny, :] - V[high, 0:ny, :])
               - CE[low, 0:ny, :] * (V[low + 1, 0:ny, :] - V[low, 0:ny, :]))
    per_lane = (jnp.sum(f_total + x_total, axis=0, keepdims=True)
                + (y_total[ny - 1:ny] - y_total[Y - 1:Y]))
    GS[iy, ix] = jnp.broadcast_to(jnp.sum(per_lane, axis=1, keepdims=True), (1, 128))
    run(sum_x, cx, "start")

    def pack(x, c):
        PLO[x] = V[H + x, 0:H, :]
        PHI[x] = V[H + x, ny - H:ny, :]
        return c

    rows_loop(0, nx, pack, 0)

    def halo2(d):
        dx, dy = DIRS[d]
        src_rows = {1: (nx - H, nx), -1: (0, H), 0: (0, nx)}[dx]
        dst_rows = {1: (0, H), -1: (X - H, X), 0: (H, H + nx)}[dx]
        if dy == 0:
            src = V.at[nx + 1:nx + H, 0:ny, :] if dx == 1 else V.at[H:H + NU, 0:ny, :]
            dst = XLO2 if dx == 1 else XHI2
        else:
            src = (PHI if dy == 1 else PLO).at[src_rows[0]:src_rows[1]]
            dst = (YLO2 if dy == 1 else YHI2).at[dst_rows[0]:dst_rows[1]]
        return pltpu.make_async_remote_copy(
            src_ref=src, dst_ref=dst, send_sem=ssem2.at[d], recv_sem=rsem2.at[d],
            device_id=(ix + dx, iy + dy), device_id_type=MESH)

    for d in range(8):
        each(d, 1, lambda d=d: halo2(d).start())

    run(coef_y, cy, "wait_recv")
    row_y = lax.broadcasted_iota(jnp.int32, (cy, 128), 0)
    diag = [GC[:, x, 0, :] for x in range(cx)]
    east = [GC[:, x, 1, :] for x in range(cx - 1)]
    north = [jnp.where(row_y < cy - 1, GC[:, x, 2, :], 0.0) for x in range(cx)]
    south = [pltpu.roll(n, 1, 0) for n in north]

    run(sum_x, cx, "wait_recv")
    run(sum_y, cy, "start")
    run(sum_y, cy, "wait_recv")
    coarse_source = [GS[:, x, 0, :] for x in range(cx)]

    def dot(a, b):
        total = a[0] * b[0]
        for x in range(1, cx):
            total = total + a[x] * b[x]
        return jnp.sum(total, axis=0, keepdims=True)

    def coarse_apply(p):
        product = []
        for x in range(cx):
            v = diag[x] * p[x] - north[x] * pltpu.roll(p[x], cy - 1, 0) - south[x] * pltpu.roll(p[x], 1, 0)
            if x < cx - 1:
                v = v - east[x] * p[x + 1]
            if x > 0:
                v = v - east[x - 1] * p[x - 1]
            product.append(v)
        return product

    def iterate_once(counter, carried):
        estimate, remainder, search, norm_now = carried
        product = coarse_apply(search)
        alpha = norm_now / dot(search, product)
        estimate = [e + alpha * s for e, s in zip(estimate, search)]
        remainder = [r - alpha * q for r, q in zip(remainder, product)]
        norm_next = dot(remainder, remainder)
        beta = norm_next / norm_now
        search = [r + beta * s for r, s in zip(remainder, search)]
        return estimate, remainder, search, norm_next

    state = ([jnp.zeros((cy, 128), jnp.float32)] * cx, coarse_source, coarse_source,
             dot(coarse_source, coarse_source))
    estimate = lax.fori_loop(0, CG_ITERS, iterate_once, state)[0]
    for x in range(cx):
        E[x] = estimate[x]

    ring = lax.broadcasted_iota(jnp.int32, (Y, 128), 0)

    def share(dx):
        def one(dy):
            jx, jy = ix + dx, iy + dy
            row = E[jnp.clip(jx, 0, cx - 1), pl.ds(jnp.clip(jy, 0, cy - 1), 1), :]
            keep = inside(jx, jy, cx, cy).astype(jnp.float32)
            return jnp.broadcast_to(row * keep, (Y, 128))
        return jnp.where(ring < ny, one(0), jnp.where(ring < ny + H, one(1), one(-1)))

    shares = {dx: share(dx) for dx in (-1, 0, 1)}

    for d in range(8):
        each(d, -1, lambda d=d: halo2(d).wait_recv())
    for d in range(8):
        each(d, 1, lambda d=d: halo2(d).wait_send())

    def edge(x, dx):
        V[x, ny:ny + H, :] = YHI2[x]
        V[x, ny + H:Y, :] = YLO2[x]
        V[x] = V[x] + shares[dx]

    for i in range(NU):
        V[1 + i, 0:ny, :] = XLO2[i]
        V[X - H + i, 0:ny, :] = XHI2[i]
    for i in range(NU):
        edge(1 + i, -1)
        edge(X - H + i, 1)

    def middle(x, c):
        edge(x, 0)
        return c

    rows_loop(H, H + nx, middle, 0)

    sweep(V, U, 2, X - 2)
    sweep(U, V, 3, X - 3)
    sweep(V, U, 4, X - 4)
    back = pltpu.make_async_copy(U.at[H:H + nx, 0:ny, :], out, osem)
    back.start()

    for d in range(8):
        def sent(d=d):
            for a in range(3):
                halo(a, d).wait_send()
        each(d, 1, sent)
    run(coef_x, cx, "wait_send")
    run(coef_y, cy, "wait_send")
    run(sum_x, cx, "wait_send")
    run(sum_y, cy, "wait_send")
    back.wait()


def body(conductivity, source, initial):
    nx, ny, nz = conductivity.shape
    cx, cy = lax.axis_size("gx"), lax.axis_size("gy")
    X, Y = nx + 2 * H, ny + 2 * H
    args = (conductivity, source, initial)
    quads = tuple(a.reshape(nx, ny // H, H, nz) for a in args)
    wide = pltpu.VMEM((X, Y, nz), jnp.float32)
    dma = pltpu.SemaphoreType.DMA

    def vmem(*shape):
        return pltpu.VMEM(shape, jnp.float32)

    return pl.pallas_call(
        functools.partial(kernel, cx, cy, nx, ny),
        out_shape=jax.ShapeDtypeStruct((nx, ny, nz), jnp.float32),
        in_specs=[pl.BlockSpec(memory_space=pl.ANY)] * 6,
        out_specs=pl.BlockSpec(memory_space=pl.ANY),
        scratch_shapes=[wide] * 8 + [
            vmem(3, X, H, nz), vmem(3, X, H, nz),
            vmem(NU, ny, nz), vmem(NU, ny, nz), vmem(X, H, nz), vmem(X, H, nz),
            vmem(nx, H, nz), vmem(nx, H, nz),
            vmem(cy, cx, 4, nz), vmem(cy, cx, 1, nz), vmem(cx, cy, nz),
            dma((3,)), dma,
            dma((24,)), dma((24,)), dma((8,)), dma((8,)),
            dma((cx - 1,)), dma((cx - 1,)), dma((cy - 1,)), dma((cy - 1,)),
            dma((cx - 1,)), dma((cx - 1,)), dma((cy - 1,)), dma((cy - 1,)),
        ],
        compiler_params=pltpu.CompilerParams(collective_id=0, has_side_effects=True),
        name="cycle",
    )(*args, *quads)


def solution(mesh):
    return jax.shard_map(
        body,
        mesh=mesh,
        in_specs=(P("gx", "gy", None), P("gx", "gy", None), P("gx", "gy", None)),
        out_specs=P("gx", "gy", None),
        check_vma=False,
    )
```

time: 253 us -> 45 us (0.18)
  the two profiles are of different devices: /device:TPU:12 before, /device:TPU:0 now
where the time goes in v1:
time: 45 us; the launch traced here: 44.8 us
  Pallas kernels  42.9 us (95%)
  local copies, waits for them, and re-layouts  1.87 us (4%)
    pallas_call x1, Pallas kernels, body(): pl.pallas_call(functools.partial(kernel, cx, cy, nx, ny), out_shape=jax.S...  42.9 us
    unnamed x1, local copies, waits for them, and re-layouts  1.87 us

profile of v1, /device:TPU:0, one launch (start us, length us, event | category | flops | bytes accessed | tf_op | source)
XLA Modules:
  0.0 44.8 jit_solution(12929414612803773160)
XLA Ops:
  0.0 42.9 %cycle.1 = f32[32,32,128]{2,1,0:T(8,128)} custom-call(f32[32,32,128]{2,1,0:T(8,128)} %refs_0_.1, f32[32,32,128]{2,1,0:T(8,128)} %refs_1_.1, f32[32,32,128]{2,1,0:T(8,128)} %refs_2_.1, f32[32,8,4,128]{3,2,1,0:T(4,128)} %bitcast.3, f32[32,8,4,128]{3,2,1,0:T(4,128)} %bitcast.4, f32[32,8,4,128]{3,2,1,0:T(4,128)} %bitcast.5), custom_call_target="tpu_custom_call" | custom-call | tf_op jit(solution)/shard_map/cycle/pallas_call | solution.py:388
  42.9 1.9 %copy.5 = f32[32,32,128]{2,1,0:T(8,128)} copy(f32[32,32,128]{2,1,0:T(8,128)} %cycle.1) | data formatting | bytes 1048576

commit v2 on v1

--- a/solution.py
+++ b/solution.py
@@ -10,6 +10,7 @@
 NU = 3
 CG_ITERS = 32
 H = NU + 1
+WIDTH = (NU, NU - 1, NU)
 
 relax_weight = 0.8
 MESH = pl.DeviceIdType.MESH
@@ -34,10 +35,21 @@
     return carry
 
 
+ROWS = 8
+
+
+def blocks_loop(lo, hi, block, carry):
+    count = (hi - lo) // ROWS
+    carry = lax.fori_loop(0, count, lambda i, c: block(lo + ROWS * i, c, ROWS), carry)
+    if (hi - lo) % ROWS:
+        carry = block(lo + ROWS * count, carry, (hi - lo) % ROWS)
+    return carry
+
+
 def kernel(cx, cy, nx, ny, *refs):
-    (k_in, f_in, u_in, k4, f4, u4, out,
-     K, F, U, V, CE, CN, CU, W, YLO, YHI,
-     XLO2, XHI2, YLO2, YHI2, PLO, PHI, GC, GS, E,
+    (k_in, f_in, u_in, k1, f1, u1, out,
+     K, F, U, V, CE, CN, CU, CD, W, YLO_K, YLO_F, YLO_U, YHI_K, YHI_F, YHI_U,
+     XLO2, XHI2, YLO2, YHI2, PLO, PHI, GC, GS, E, R,
      lsem, osem, ssem, rsem, ssem2, rsem2,
      c1s, c1r, c2s, c2r, s1s, s1r, s2s, s2r) = refs
     X = nx + 2 * H
@@ -45,8 +57,10 @@
     ix = lax.axis_index("gx")
     iy = lax.axis_index("gy")
     full = [k_in, f_in, u_in]
-    quad = [k4, f4, u4]
+    thin = [k1, f1, u1]
     ext = [K, F, U]
+    YLO = [YLO_K, YLO_F, YLO_U]
+    YHI = [YHI_K, YHI_F, YHI_U]
 
     barrier = pltpu.get_barrier_semaphore()
 
@@ -73,17 +87,23 @@
     sides_y = (iy > 0).astype(jnp.int32) + (iy < cy - 1).astype(jnp.int32)
     pl.semaphore_wait(barrier, (cx - 1) + (cy - 1) + sides_x * sides_y)
 
+    def spans(dx, w):
+        src = {1: (nx - w, nx), -1: (0, w), 0: (0, nx)}[dx]
+        dst = {1: (H - w, H), -1: (X - H, X - H + w), 0: (H, H + nx)}[dx]
+        return src, dst
+
     def halo(a, d):
         dx, dy = DIRS[d]
         slot = a * 8 + d
-        src_rows = {1: (nx - H, nx), -1: (0, H), 0: (0, nx)}[dx]
-        dst_rows = {1: (0, H), -1: (X - H, X), 0: (H, H + nx)}[dx]
+        w = WIDTH[a]
+        src_rows, dst_rows = spans(dx, w)
         if dy == 0:
             src = full[a].at[src_rows[0]:src_rows[1]]
             dst = ext[a].at[dst_rows[0]:dst_rows[1], 0:ny, :]
         else:
-            src = quad[a].at[src_rows[0]:src_rows[1], ny // H - 1 if dy == 1 else 0]
-            dst = (YLO if dy == 1 else YHI).at[a, dst_rows[0]:dst_rows[1]]
+            cols = (ny - w, ny) if dy == 1 else (0, w)
+            src = thin[a].at[src_rows[0]:src_rows[1], cols[0]:cols[1]]
+            dst = (YLO if dy == 1 else YHI)[a].at[dst_rows[0]:dst_rows[1]]
         return pltpu.make_async_remote_copy(
             src_ref=src, dst_ref=dst, send_sem=ssem.at[slot], recv_sem=rsem.at[slot],
             device_id=(ix + dx, iy + dy), device_id_type=MESH)
@@ -100,92 +120,27 @@
 
     def clear_when_absent(d):
         dx, dy = DIRS[d]
-        rows = {1: (0, H), -1: (X - H, X), 0: (H, H + nx)}[dx]
 
         @pl.when(jnp.logical_not(inside(ix - dx, iy - dy, cx, cy)))
         def _():
+            for a in range(3):
+                w = WIDTH[a]
+                lo, hi = spans(dx, w)[1]
+                if dy == 0:
+                    ext[a][lo:hi, 0:ny, :] = jnp.zeros((w, ny, 128), jnp.float32)
+                else:
+                    (YLO if dy == 1 else YHI)[a][lo:hi] = jnp.zeros((hi - lo, w, 1, 128), jnp.float32)
             if dy == 0:
-                for a in range(3):
-                    ext[a][rows[0]:rows[1], 0:ny, :] = jnp.zeros((H, ny, 128), jnp.float32)
                 (XLO2 if dx == 1 else XHI2)[...] = jnp.zeros((NU, ny, 128), jnp.float32)
             else:
-                wide = YLO if dy == 1 else YHI
-                wide2 = YLO2 if dy == 1 else YHI2
-                for a in range(3):
-                    wide[a, rows[0]:rows[1]] = jnp.zeros((rows[1] - rows[0], H, 128), jnp.float32)
-                wide2[rows[0]:rows[1]] = jnp.zeros((rows[1] - rows[0], H, 128), jnp.float32)
+                lo, hi = spans(dx, H)[1]
+                (YLO2 if dy == 1 else YHI2)[lo:hi] = jnp.zeros((hi - lo, H, 128), jnp.float32)
 
     for d in range(8):
         clear_when_absent(d)
 
     for copy in local:
         copy.wait()
-
-    f_total = rows_loop(H, H + nx, lambda x, c: c + F[x, 0:ny, :], jnp.zeros((ny, 128), jnp.float32))
-
-    for d in range(8):
-        def finish(d=d):
-            for a in range(3):
-                halo(a, d).wait_recv()
-        each(d, -1, finish)
-
-    def unpack(x, c):
-        for a in range(3):
-            ext[a][x, ny:ny + H, :] = YHI[a, x]
-            ext[a][x, ny + H:Y, :] = YLO[a, x]
-        return c
-
-    rows_loop(0, X, unpack, 0)
-
-    lane = lax.broadcasted_iota(jnp.int32, (Y, 128), 1)
-    up_half = jnp.where(lane < 127, 0.5, 0.0)
-
-    def next_y(v):
-        return pltpu.roll(v, Y - 1, 0)
-
-    def last_y(v):
-        return pltpu.roll(v, 1, 0)
-
-    def next_z(v):
-        return pltpu.roll(v, 127, 1)
-
-    def last_z(v):
-        return pltpu.roll(v, 1, 1)
-
-    def faces(x, c):
-        k, west, total = c
-        k_next = K[x + 1]
-        east = 0.5 * (k + k_next)
-        north = 0.5 * (k + next_y(k))
-        up = up_half * (k + next_z(k))
-        d = east + west + north + last_y(north) + up + last_z(up)
-        CE[x] = east
-        CN[x] = north
-        CU[x] = up
-        W[x] = jnp.where(k > 0, relax_weight / jnp.where(k > 0, d, 1.0), 0.0)
-        return k_next, east, total + north
-
-    k1 = K[1]
-    first = 0.5 * (K[0] + k1)
-    CE[0] = first
-    zero = jnp.zeros((Y, 128), jnp.float32)
-    carry = rows_loop(1, H, faces, (k1, first, zero))
-    carry = rows_loop(H, H + nx, faces, (carry[0], carry[1], zero))
-    north_total = carry[2]
-    rows_loop(H + nx, X - 1, faces, carry)
-
-    def whole_sum(v):
-        return jnp.sum(jnp.sum(v, axis=0, keepdims=True), axis=1, keepdims=True)
-
-    flow_e = whole_sum(CE[X - H - 1, 0:ny, :])
-    flow_w = whole_sum(CE[H - 1, 0:ny, :])
-    flow_n = whole_sum(north_total[ny - 1:ny])
-    flow_s = whole_sum(north_total[Y - 1:Y])
-    coarse_diag = flow_e + flow_w + flow_n + flow_s
-    GC[iy, ix, 0:1, :] = jnp.broadcast_to(coarse_diag, (1, 128))
-    GC[iy, ix, 1:2, :] = jnp.broadcast_to(flow_e, (1, 128))
-    GC[iy, ix, 2:3, :] = jnp.broadcast_to(flow_n, (1, 128))
-    GC[iy, ix, 3:4, :] = jnp.zeros((1, 128), jnp.float32)
 
     def along_x(G, ss, rs):
         def of(k):
@@ -209,45 +164,118 @@
 
     coef_x, coef_y = along_x(GC, c1s, c1r), along_y(GC, c2s, c2r)
     sum_x, sum_y = along_x(GS, s1s, s1r), along_y(GS, s2s, s2r)
+
+    lane_row = lax.broadcasted_iota(jnp.int32, (1, 128), 1)
+
+    def whole(v):
+        return jnp.sum(jnp.sum(v, axis=0, keepdims=True), axis=1, keepdims=True)
+
+    def in_lanes(values):
+        row = jnp.zeros((1, 128), jnp.float32)
+        for k, v in enumerate(values):
+            row = jnp.where(lane_row == k, v, row)
+        return row
+
+    def outer(x, c):
+        return c[0] + K[x, 0:1, :], c[1] + K[x, ny - 1:ny, :]
+
+    none = jnp.zeros((1, 128), jnp.float32)
+    y_first, y_last = rows_loop(H, H + nx, outer, (none, none))
+    GC[iy, ix] = in_lanes([whole(K[H, 0:ny, :]), whole(K[H + nx - 1, 0:ny, :]), whole(y_first), whole(y_last)])
     run(coef_x, cx, "start")
-
-    def sweep(src, dst, lo, hi, final=None):
-        def step(x, c):
-            u, west, total = c
-            u_next = src[x + 1]
-            east = CE[x] * (u_next - u)
-            cn = CN[x]
-            north = cn * (next_y(u) - u)
-            up = CU[x] * (next_z(u) - u)
-            change = (east - west) + (north - last_y(north)) + (up - last_z(up))
-            new = u + W[x] * (F[x] + change)
-            dst[x] = new
-            if final is not None:
-                total = total + cn * (next_y(new) - new)
-            return u_next, east, total
-        u = src[lo]
-        west = CE[lo - 1] * (u - src[lo - 1])
-        zero = jnp.zeros((Y, 128), jnp.float32) if final is not None else 0
-        if final is None:
-            rows_loop(lo, hi, step, (u, west, zero))
-            return None
-        carry = rows_loop(lo, final[0], step, (u, west, zero))
-        carry = rows_loop(final[0], final[1], step, (carry[0], carry[1], zero))
-        rows_loop(final[1], hi, step, carry)
-        return carry[2]
-
-    sweep(U, V, 1, X - 1)
+    f_total = rows_loop(H, H + nx, lambda x, c: c + F[x, 0:ny, :], jnp.zeros((ny, 128), jnp.float32))
+    f_total = jnp.sum(f_total, axis=0, keepdims=True)
+
     run(coef_x, cx, "wait_recv")
     run(coef_y, cy, "start")
-    sweep(V, U, 2, X - 2)
-    y_total = sweep(U, V, 3, X - 3, (H, H + nx))
-
-    low, high = H - 1, X - H - 1
-    x_total = (CE[high, 0:ny, :] * (V[high + 1, 0:ny, :] - V[high, 0:ny, :])
-               - CE[low, 0:ny, :] * (V[low + 1, 0:ny, :] - V[low, 0:ny, :]))
-    per_lane = (jnp.sum(f_total + x_total, axis=0, keepdims=True)
-                + (y_total[ny - 1:ny] - y_total[Y - 1:Y]))
-    GS[iy, ix] = jnp.broadcast_to(jnp.sum(per_lane, axis=1, keepdims=True), (1, 128))
+
+    for d in range(8):
+        def finish(d=d):
+            for a in range(3):
+                halo(a, d).wait_recv()
+        each(d, -1, finish)
+
+    def unpack(x, c):
+        for a in range(3):
+            w = WIDTH[a]
+            ext[a][x, ny:ny + w, :] = YHI[a][x, :, 0, :]
+            ext[a][x, Y - w:Y, :] = YLO[a][x, :, 0, :]
+        return c
+
+    rows_loop(1, X - 1, unpack, 0)
+
+    lane = lax.broadcasted_iota(jnp.int32, (Y, 128), 1)
+    up_half = jnp.where(lane < 127, 0.5, 0.0)
+    down_half = jnp.where(lane > 0, 0.5, 0.0)
+
+    def next_y(v):
+        return pltpu.roll(v, Y - 1, 0)
+
+    def last_y(v):
+        return pltpu.roll(v, 1, 0)
+
+    def next_z(v):
+        return pltpu.roll(v, 127, 1)
+
+    def last_z(v):
+        return pltpu.roll(v, 1, 1)
+
+    def faces(x, c, rows):
+        k, west = c
+        ks = [k] + [K[x + 1 + r] for r in range(rows)]
+        ups = [next_z(ks[r]) for r in range(rows)]
+        downs = [last_z(ks[r]) for r in range(rows)]
+        for r in range(rows):
+            k = ks[r]
+            east = 0.5 * (k + ks[r + 1])
+            north = 0.5 * (k + next_y(k))
+            up = up_half * (k + ups[r])
+            down = down_half * (k + downs[r])
+            d = east + west + north + last_y(north) + up + down
+            CE[x + r] = east
+            CN[x + r] = north
+            CU[x + r] = up
+            CD[x + r] = down
+            W[x + r] = jnp.where(k > 0, relax_weight / jnp.where(k > 0, d, 1.0), 0.0)
+            west = east
+        return ks[rows], west
+
+    zero = jnp.zeros((Y, 128), jnp.float32)
+    CE[1] = 0.5 * (K[1] + K[2])
+    blocks_loop(2, X - 2, faces, (K[2], CE[1]))
+
+    def sweep(src, dst, lo, hi, final=False):
+        def block(x, c, rows):
+            u, west, low, high = c
+            us = [u] + [src[x + 1 + r] for r in range(rows)]
+            ups = [next_z(us[r]) for r in range(rows)]
+            downs = [last_z(us[r]) for r in range(rows)]
+            for r in range(rows):
+                u = us[r]
+                east = CE[x + r] * (us[r + 1] - u)
+                cn = CN[x + r]
+                north = cn * (next_y(u) - u)
+                change = ((east - west) + (north - last_y(north))
+                          + (CU[x + r] * (ups[r] - u) + CD[x + r] * (downs[r] - u)))
+                new = u + W[x + r] * (F[x + r] + change)
+                dst[x + r] = new
+                if final:
+                    low, high = low + cn[Y - 1:Y] * new[0:1], high + cn[ny - 1:ny] * new[ny - 1:ny]
+                west = east
+            return us[rows], west, low, high
+
+        start = (src[lo], CE[lo - 1] * (src[lo] - src[lo - 1]))
+        start += (none, none) if final else (0, 0)
+        return blocks_loop(lo, hi, block, start)[2:]
+
+    sweep(U, V, 2, X - 2)
+    sweep(V, U, 3, X - 3)
+    y_low, y_high = sweep(U, V, 4, X - 4, True)
+
+    x_low = jnp.sum(CE[H - 1, 0:ny, :] * V[H, 0:ny, :], axis=0, keepdims=True)
+    x_high = jnp.sum(CE[X - H - 1, 0:ny, :] * V[X - H - 1, 0:ny, :], axis=0, keepdims=True)
+    own = f_total - x_low - x_high - y_low - y_high
+    GS[iy, ix] = in_lanes([jnp.sum(v, axis=1, keepdims=True) for v in (own, x_low, x_high, y_low, y_high)])
     run(sum_x, cx, "start")
 
     def pack(x, c):
@@ -271,20 +299,46 @@
             src_ref=src, dst_ref=dst, send_sem=ssem2.at[d], recv_sem=rsem2.at[d],
             device_id=(ix + dx, iy + dy), device_id_type=MESH)
 
-    for d in range(8):
-        each(d, 1, lambda d=d: halo2(d).start())
-
     run(coef_y, cy, "wait_recv")
     row_y = lax.broadcasted_iota(jnp.int32, (cy, 128), 0)
-    diag = [GC[:, x, 0, :] for x in range(cx)]
-    east = [GC[:, x, 1, :] for x in range(cx - 1)]
-    north = [jnp.where(row_y < cy - 1, GC[:, x, 2, :], 0.0) for x in range(cx)]
+
+    def tidy(G, k):
+        for x in range(cx):
+            for y in range(cy):
+                R[k, x, y:y + 1, :] = G[y, x]
+        return [R[k, x] for x in range(cx)]
+
+    def lane_of(rows, k):
+        return [jnp.broadcast_to(r[:, k:k + 1], (cy, 128)) for r in rows]
+
+    def after_y(v):
+        return jnp.where(row_y < cy - 1, pltpu.roll(v, cy - 1, 0), 0.0)
+
+    def before_y(v):
+        return jnp.where(row_y > 0, pltpu.roll(v, 1, 0), 0.0)
+
+    coarse_rows = tidy(GC, 0)
+    nil = jnp.zeros((cy, 128), jnp.float32)
+    x_first, x_last, y_first, y_last = [lane_of(coarse_rows, k) for k in range(4)]
+    east = [0.5 * (a + b) for a, b in zip(x_last, x_first[1:] + [nil])]
+    west = [0.5 * (a + b) for a, b in zip(x_first, [nil] + x_last[:-1])]
+    north = [0.5 * (a + after_y(b)) for a, b in zip(y_last, y_first)]
+    south = [0.5 * (a + before_y(b)) for a, b in zip(y_first, y_last)]
+    diag = [a + b + c + d for a, b, c, d in zip(east, west, north, south)]
+    north = [jnp.where(row_y < cy - 1, n, 0.0) for n in north]
     south = [pltpu.roll(n, 1, 0) for n in north]
 
     run(sum_x, cx, "wait_recv")
     run(sum_y, cy, "start")
+    for d in range(8):
+        each(d, 1, lambda d=d: halo2(d).start())
+
     run(sum_y, cy, "wait_recv")
-    coarse_source = [GS[:, x, 0, :] for x in range(cx)]
+    coarse_rows = tidy(GS, 1)
+    own, x_low, x_high, y_low, y_high = [lane_of(coarse_rows, k) for k in range(5)]
+    coarse_source = [
+        (a + after_y(b)) + (before_y(c) + d + e)
+        for a, b, c, d, e in zip(own, y_low, y_high, x_low[1:] + [nil], [nil] + x_high[:-1])]
 
     def dot(a, b):
         total = a[0] * b[0]
@@ -378,7 +432,7 @@
     cx, cy = lax.axis_size("gx"), lax.axis_size("gy")
     X, Y = nx + 2 * H, ny + 2 * H
     args = (conductivity, source, initial)
-    quads = tuple(a.reshape(nx, ny // H, H, nz) for a in args)
+    thin = tuple(a.reshape(nx, ny, 1, nz) for a in args)
     wide = pltpu.VMEM((X, Y, nz), jnp.float32)
     dma = pltpu.SemaphoreType.DMA
 
@@ -388,13 +442,13 @@
     return pl.pallas_call(
         functools.partial(kernel, cx, cy, nx, ny),
         out_shape=jax.ShapeDtypeStruct((nx, ny, nz), jnp.float32),
-        in_specs=[pl.BlockSpec(memory_space=pl.ANY)] * 6,
+        in_specs=[pl.BlockSpec(memory_space=pltpu.HBM)] * 6,
         out_specs=pl.BlockSpec(memory_space=pl.ANY),
-        scratch_shapes=[wide] * 8 + [
-            vmem(3, X, H, nz), vmem(3, X, H, nz),
+        scratch_shapes=[wide] * 9 + [
+            *[vmem(X, w, 1, nz) for w in WIDTH + WIDTH],
             vmem(NU, ny, nz), vmem(NU, ny, nz), vmem(X, H, nz), vmem(X, H, nz),
             vmem(nx, H, nz), vmem(nx, H, nz),
-            vmem(cy, cx, 4, nz), vmem(cy, cx, 1, nz), vmem(cx, cy, nz),
+            vmem(cy, cx, 1, nz), vmem(cy, cx, 1, nz), vmem(cx, cy, nz), vmem(2, cx, cy, nz),
             dma((3,)), dma,
             dma((24,)), dma((24,)), dma((8,)), dma((8,)),
             dma((cx - 1,)), dma((cx - 1,)), dma((cy - 1,)), dma((cy - 1,)),
@@ -402,7 +456,7 @@
         ],
         compiler_params=pltpu.CompilerParams(collective_id=0, has_side_effects=True),
         name="cycle",
-    )(*args, *quads)
+    )(*args, *thin)
 
 
 def solution(mesh):

time: 45 us -> 29.2 us (0.65)
  Pallas kernels: 42.9 us -> 27.1 us
    pallas_call x1, Pallas kernels: 42.9 us -> 27.1 us  [body(): pl.pallas_call(functools.partial(kernel, cx, cy, nx, ny), out_shape=jax.S...]
where the time goes in v2:
time: 29.2 us; the launch traced here: 29 us
  Pallas kernels  27.1 us (93%)
  local copies, waits for them, and re-layouts  1.87 us (6%)
    pallas_call x1, Pallas kernels, body(): pl.pallas_call(functools.partial(kernel, cx, cy, nx, ny), out_shape=jax.S...  27.1 us
    unnamed x1, local copies, waits for them, and re-layouts  1.87 us

profile of v2, /device:TPU:0, one launch (start us, length us, event | category | flops | bytes accessed | tf_op | source)
XLA Modules:
  0.0 29.0 jit_solution(454331576016624375)
XLA Ops:
  0.0 27.1 %cycle.1 = f32[32,32,128]{2,1,0:T(8,128)} custom-call(f32[32,32,128]{2,1,0:T(8,128)} %refs_0_.1, f32[32,32,128]{2,1,0:T(8,128)} %refs_1_.1, f32[32,32,128]{2,1,0:T(8,128)} %refs_2_.1, f32[32,32,1,128]{3,2,1,0:T(1,128)} %bitcast.3, f32[32,32,1,128]{3,2,1,0:T(1,128)} %bitcast.4, f32[32,32,1,128]{3,2,1,0:T(1,128)} %bitcast.5), custom_call_target="tpu_custom_call" | custom-call | tf_op jit(solution)/shard_map/cycle/pallas_call | solution.py:442
  27.1 1.9 %copy.5 = f32[32,32,128]{2,1,0:T(8,128)} copy(f32[32,32,128]{2,1,0:T(8,128)} %cycle.1) | data formatting | bytes 1048576

commit v3 on v2

--- a/solution.py
+++ b/solution.py
@@ -36,6 +36,7 @@
 
 
 ROWS = 8
+DIRECT = 64
 
 
 def blocks_loop(lo, hi, block, carry):
@@ -51,7 +52,7 @@
      K, F, U, V, CE, CN, CU, CD, W, YLO_K, YLO_F, YLO_U, YHI_K, YHI_F, YHI_U,
      XLO2, XHI2, YLO2, YHI2, PLO, PHI, GC, GS, E, R,
      lsem, osem, ssem, rsem, ssem2, rsem2,
-     c1s, c1r, c2s, c2r, s1s, s1r, s2s, s2r) = refs
+     c1s, c1r, c2s, c2r, s1s, s1r, s2s, s2r, das, dar) = refs
     X = nx + 2 * H
     Y = ny + 2 * H
     ix = lax.axis_index("gx")
@@ -155,6 +156,14 @@
                 src_ref=G.at[iy], dst_ref=G.at[iy], send_sem=ss.at[k - 1], recv_sem=rs.at[k - 1],
                 device_id=(ix, lax.rem(iy + k, cy)), device_id_type=MESH)
         return of
+
+    def to_all(k):
+        target = lax.rem(ix * cy + iy + k, cx * cy)
+        return pltpu.make_async_remote_copy(
+            src_ref=GS.at[iy, ix], dst_ref=GS.at[iy, ix], send_sem=das.at[k - 1], recv_sem=dar.at[k - 1],
+            device_id=(target // cy, lax.rem(target, cy)), device_id_type=MESH)
+
+    direct = cx * cy <= DIRECT
 
     def run(of, count, method):
         def go(k, c):
@@ -276,7 +285,12 @@
     x_high = jnp.sum(CE[X - H - 1, 0:ny, :] * V[X - H - 1, 0:ny, :], axis=0, keepdims=True)
     own = f_total - x_low - x_high - y_low - y_high
     GS[iy, ix] = in_lanes([jnp.sum(v, axis=1, keepdims=True) for v in (own, x_low, x_high, y_low, y_high)])
-    run(sum_x, cx, "start")
+    if direct:
+        run(coef_y, cy, "wait_recv")
+        run(to_all, cx * cy, "start")
+    else:
+        run(sum_x, cx, "start")
+        run(coef_y, cy, "wait_recv")
 
     def pack(x, c):
         PLO[x] = V[H + x, 0:H, :]
@@ -299,7 +313,6 @@
             src_ref=src, dst_ref=dst, send_sem=ssem2.at[d], recv_sem=rsem2.at[d],
             device_id=(ix + dx, iy + dy), device_id_type=MESH)
 
-    run(coef_y, cy, "wait_recv")
     row_y = lax.broadcasted_iota(jnp.int32, (cy, 128), 0)
 
     def tidy(G, k):
@@ -328,12 +341,12 @@
     north = [jnp.where(row_y < cy - 1, n, 0.0) for n in north]
     south = [pltpu.roll(n, 1, 0) for n in north]
 
-    run(sum_x, cx, "wait_recv")
-    run(sum_y, cy, "start")
+    if not direct:
+        run(sum_x, cx, "wait_recv")
+        run(sum_y, cy, "start")
     for d in range(8):
         each(d, 1, lambda d=d: halo2(d).start())
-
-    run(sum_y, cy, "wait_recv")
+    run(*((to_all, cx * cy) if direct else (sum_y, cy)), "wait_recv")
     coarse_rows = tidy(GS, 1)
     own, x_low, x_high, y_low, y_high = [lane_of(coarse_rows, k) for k in range(5)]
     coarse_source = [
@@ -411,9 +424,13 @@
 
     sweep(V, U, 2, X - 2)
     sweep(U, V, 3, X - 3)
-    sweep(V, U, 4, X - 4)
-    back = pltpu.make_async_copy(U.at[H:H + nx, 0:ny, :], out, osem)
-    back.start()
+    half = nx // 2
+    back = [pltpu.make_async_copy(U.at[H + r:H + r + half, 0:ny, :], out.at[r:r + half], osem.at[i])
+            for i, r in enumerate((0, half))]
+    sweep(V, U, H, H + half)
+    back[0].start()
+    sweep(V, U, H + half, H + nx)
+    back[1].start()
 
     for d in range(8):
         def sent(d=d):
@@ -422,9 +439,13 @@
         each(d, 1, sent)
     run(coef_x, cx, "wait_send")
     run(coef_y, cy, "wait_send")
-    run(sum_x, cx, "wait_send")
-    run(sum_y, cy, "wait_send")
-    back.wait()
+    if direct:
+        run(to_all, cx * cy, "wait_send")
+    else:
+        run(sum_x, cx, "wait_send")
+        run(sum_y, cy, "wait_send")
+    for copy in back:
+        copy.wait()
 
 
 def body(conductivity, source, initial):
@@ -449,10 +470,11 @@
             vmem(NU, ny, nz), vmem(NU, ny, nz), vmem(X, H, nz), vmem(X, H, nz),
             vmem(nx, H, nz), vmem(nx, H, nz),
             vmem(cy, cx, 1, nz), vmem(cy, cx, 1, nz), vmem(cx, cy, nz), vmem(2, cx, cy, nz),
-            dma((3,)), dma,
+            dma((3,)), dma((2,)),
             dma((24,)), dma((24,)), dma((8,)), dma((8,)),
             dma((cx - 1,)), dma((cx - 1,)), dma((cy - 1,)), dma((cy - 1,)),
             dma((cx - 1,)), dma((cx - 1,)), dma((cy - 1,)), dma((cy - 1,)),
+            dma((min(cx * cy, DIRECT) - 1,)), dma((min(cx * cy, DIRECT) - 1,)),
         ],
         compiler_params=pltpu.CompilerParams(collective_id=0, has_side_effects=True),
         name="cycle",

time: 29.2 us -> 27.7 us (0.949)
  Pallas kernels: 27.1 us -> 25.7 us
    pallas_call x1, Pallas kernels: 27.1 us -> 25.7 us  [body(): pl.pallas_call(functools.partial(kernel, cx, cy, nx, ny), out_shape=jax.S...]
where the time goes in v3:
time: 27.7 us; the launch traced here: 27.6 us
  Pallas kernels  25.7 us (93%)
  local copies, waits for them, and re-layouts  1.87 us (7%)
    pallas_call x1, Pallas kernels, body(): pl.pallas_call(functools.partial(kernel, cx, cy, nx, ny), out_shape=jax.S...  25.7 us
    unnamed x1, local copies, waits for them, and re-layouts  1.87 us

profile of v3, /device:TPU:0, one launch (start us, length us, event | category | flops | bytes accessed | tf_op | source)
XLA Modules:
  0.0 27.6 jit_solution(11883882193509598374)
XLA Ops:
  0.0 25.7 %cycle.1 = f32[32,32,128]{2,1,0:T(8,128)} custom-call(f32[32,32,128]{2,1,0:T(8,128)} %refs_0_.1, f32[32,32,128]{2,1,0:T(8,128)} %refs_1_.1, f32[32,32,128]{2,1,0:T(8,128)} %refs_2_.1, f32[32,32,1,128]{3,2,1,0:T(1,128)} %bitcast.3, f32[32,32,1,128]{3,2,1,0:T(1,128)} %bitcast.4, f32[32,32,1,128]{3,2,1,0:T(1,128)} %bitcast.5), custom_call_target="tpu_custom_call" | custom-call | tf_op jit(solution)/shard_map/cycle/pallas_call | solution.py:463
  25.7 1.9 %copy.5 = f32[32,32,128]{2,1,0:T(8,128)} copy(f32[32,32,128]{2,1,0:T(8,128)} %cycle.1) | data formatting | bytes 1048576
